TPU v7x, 32 devices: a whole 2x2x4 slice. The times are simulated.
32 devices in a mesh: stem: 8 (over y, x, core), grp: 4 (over z).
Axes of the slice: x: 2, y: 2, z: 4, core: 2. Of those that a mesh axis runs over, the one named last changes fastest.
Arguments:
- stem_tensor: float32 [32, 512, 512], P(None, 'stem', 'grp'), may hold values from -6 to 6
- left_factors: float32 [2, 16, 16, 256], P(None, 'grp'), may hold values from -0.375 to 0.375
- right_factors: float32 [2, 256, 1024], replicated, may hold values from -0.1875 to 0.1875
- index_labels: int32 [2, 9], replicated, may hold values from 0 to 8, each once within a row
Outputs:
- contracted: float32 [32, 512, 512], P(('stem', 'grp'))
Inputs may be any that keep to these rules, and one draw needn't show every extreme that they name: `index_labels`: each row is a permutation of 0 to 8.
All inputs are finite; a program needn't handle non-finite values.
Results may differ from a plain program's by a relative error of at most 0.000098.
Values sent between devices are 32-bit elements; how exact they have to be, the bound alone decides.
No kernel may reach another device: no remote copies, remote signals or barrier semaphores. Data moves between devices by JAX's collectives and lax.ppermute only.
A program may use at most 64 MiB of HBM per device.

v0:
```python
import jax
import jax.numpy as jnp
from jax import lax
from jax.sharding import PartitionSpec as P

LOW = 32


def assemble(left, right):
    upper = left.shape[1]
    table = right.reshape(right.shape[0], LOW, LOW)
    product = jnp.einsum("abk,kcd->acbd", left, table, precision=lax.Precision.HIGHEST)
    return product.reshape(left.shape[0] * LOW, upper * LOW)


def relabel(branch, bit_order):
    row_ids = jnp.arange(branch.shape[0], dtype=jnp.int32)
    source_rows = jnp.zeros_like(row_ids)
    for bit_number in range(bit_order.shape[0]):
        picked = jnp.bitwise_and(jnp.right_shift(row_ids, bit_number), 1)
        source_rows = source_rows + jnp.left_shift(picked, bit_order[bit_number])
    return jnp.take(branch, source_rows, axis=0)


def contract_last(tensor, branch):
    dims = tensor.shape
    flat = jnp.dot(tensor.reshape(-1, dims[-1]), branch, precision=lax.Precision.HIGHEST)
    return flat.reshape(dims[:-1] + (branch.shape[1],))


def on_device(stem_tensor, left_factors, right_factors, index_labels):
    whole_left = lax.all_gather(left_factors, "grp", axis=1, tiled=True)
    branches = jnp.stack(
        [assemble(whole_left[branch_id], right_factors[branch_id]) for branch_id in range(2)]
    )
    branch_one = relabel(branches[0], index_labels[0])
    branch_two = relabel(branches[1], index_labels[1])
    stem_count = lax.axis_size("stem")
    open_rows, outer_local, inner_local = stem_tensor.shape
    shaped = stem_tensor.reshape(stem_count, open_rows // stem_count, outer_local, inner_local)
    regrouped = lax.all_to_all(shaped, "grp", split_axis=1, concat_axis=3, tiled=True)
    halfway = contract_last(regrouped, branch_one)
    gathered_modes = lax.all_to_all(halfway, "stem", split_axis=0, concat_axis=2, tiled=True)
    slab = gathered_modes[0]
    return lax.dot_general(
        slab, branch_two, (((1,), (0,)), ((), ())), precision=lax.Precision.HIGHEST
    )


def solution(mesh):
    placed = (P(None, "stem", "grp"), P(None, "grp", None, None), P(), P())
    return jax.shard_map(
        on_device,
        mesh=mesh,
        in_specs=placed,
        out_specs=P(("stem", "grp"), None, None),
        check_vma=False,
    )
```

profile of v0, /device:TPU:0, one launch (start us, length us, event | category | flops | bytes accessed | tf_op | source)
XLA Modules:
  0.0 91.7 jit_solution(12908365413325150748)
XLA Ops:
  0.0 2.3 %copy.20 = f32[8,4,64,128]{3,2,0,1:T(8,128)} copy(f32[8,4,64,128]{3,2,1,0:T(8,128)} %bitcast.70) | data formatting | bytes 2097152 | tf_op jit(solution)/shard_map/reshape | solution.py:40
  2.3 0.0 copy-start.2
  2.3 6.5 %all-to-all-start = ((f32[8,4,64,128]{3,2,0,1:T(8,128)}), f32[8,4,64,128]{3,2,0,1:T(8,128)S(1)}, u32[]{:S(2)}, u32[]{:S(2)}) async-start(f32[8,4,64,128]{3,2,0,1:T(8,128)} %copy.20), calls=%async_computation | async-start | bytes 2097152 | tf_op jit(solution)/shard_map/all_to_all | solution.py:41
  8.8 2.7 %fusion.11 = (f32[1,256,1024]{2,1,0:T(8,128)}, f32[1,256,1024]{2,1,0:T(8,128)S(1)}) fusion(f32[2,256,1024]{2,1,0:T(8,128)} %param.8), kind=kLoop, calls=%fused_computation.33 | loop fusion | bytes 4194304 | tf_op jit(solution)/shard_map/slice | solution.py:34
  11.5 0.3 copy.18
  11.8 0.0 copy-done.2
  11.8 33.1 %all_gather.3 = f32[2,16,16,256]{3,2,1,0:T(8,128)S(1)} all-gather(f32[2,4,16,256]{3,2,1,0:T(8,128)S(1)} %copy-done.2), channel_id=1, replica_groups=mesh['stem'=8,'grp'=4] {'grp'}, dimensions={1}, use_global_device_ids=true | all-gather | bytes 655360 | tf_op jit(solution)/shard_map/all_gather | solution.py:32
  44.9 0.0 copy-start.1
  44.9 0.8 copy-done.1
  45.7 3.4 %convolution_bitcast_fusion.1 = f32[16,32,16,32]{3,2,0,1:T(8,128)S(1)} fusion(f32[256,32,32,1]{0,2,3,1:T(8,128)S(1)} %bitcast.68, f32[2,16,16,256]{3,2,1,0:T(8,128)S(1)} %all_gather.3), kind=kOutput, calls=%fused_computation.3 | convolution fusion | flops 805306368 | bytes 2359296 | tf_op jit(solution)/shard_map/abk,kcd->acbd/dot_general | solution.py:12
  49.2 2.4 %copy.19 = f32[16,32,16,32]{3,2,1,0:T(8,128)} copy(f32[16,32,16,32]{3,2,0,1:T(8,128)S(1)} %convolution_bitcast_fusion.1) | data formatting | bytes 2097152 | tf_op jit(solution)/shard_map/abk,kcd->acbd/transpose | solution.py:12
  51.6 0.0 copy-start.3
  51.6 3.6 %squeeze_stack_reshape.6 = f32[512,512]{1,0:T(8,128)S(1)} reshape(f32[16,32,16,32]{3,2,1,0:T(8,128)} %copy.19) | data formatting | bytes 2097152 | tf_op jit(solution)/shard_map/squeeze;stack;reshape | solution.py:36
  55.1 0.0 copy-done.3
  55.2 0.7 fusion.12
  55.9 5.6 %compare_and_fusion.1 = (pred[512]{0:T(512)(128)(4,1)S(1)}, s32[512]{0:T(512)S(1)}) fusion(s32[]{:T(128)} %bitcast.8, s32[]{:T(128)} %bitcast.7, s32[]{:T(128)} %bitcast.6, s32[]{:T(128)} %bitcast.5, s32[]{:T(128)} %bitcast.4, s32[]{:T(128)} %bitcast.3, s32[]{:T(128)} %bitcast.2, s32[]{:T(128)} %bitcast.1, s32[]{:T(128)} %bitcast), kind=kLoop, calls=%fused_computation.30 | loop fusion | flops 20992 | bytes 2596 | tf_op jit(solution)/shard_map/jit(_take)/and | solution.py:22
  61.5 1.6 %gather_fusion = f32[512,512]{1,0:T(8,128)S(1)} fusion(f32[512,512]{1,0:T(8,128)S(1)} %squeeze_stack_reshape.6, s32[1024]{0:T(1024)S(1)} %pad_clamp_fusion.1), kind=kCustom, calls=%fused_computation.clone | custom fusion | bytes 2099200 | tf_op jit(solution)/shard_map/jit(_take)/gather | solution.py:22
  63.2 0.0 copy-start
  63.2 0.0 all-to-all-done
  63.2 0.7 copy.21
  63.9 3.0 %fusion = f32[512,512]{0,1:T(8,128)} fusion(f32[64,8,4,128]{3,2,1,0:T(4,128)S(1)} %bitcast.67, f32[512,512]{1,0:T(8,128)S(1)} %gather_fusion, pred[512]{0:T(512)(128)(4,1)S(1)} %get-tuple-element.8), kind=kOutput, calls=%fused_computation.5 | convolution fusion | flops 1610874880 | bytes 3146240 | tf_op jit(solution)/shard_map/dot_general | solution.py:27
  66.9 3.7 %all-to-all-start.1 = ((f32[8,1,64,512]{3,2,1,0:T(8,128)}), f32[8,1,64,512]{3,2,1,0:T(8,128)S(1)}, u32[]{:S(2)}, u32[]{:S(2)}) async-start(f32[8,1,64,512]{3,2,1,0:T(8,128)} %bitcast.20), calls=%async_computation.1 | async-start | bytes 2097152 | tf_op jit(solution)/shard_map/all_to_all | solution.py:43
  70.6 0.0 copy-done
  70.6 0.3 copy.23
  71.0 4.4 %convolution_bitcast_fusion = f32[16,32,16,32]{3,2,0,1:T(8,128)S(1)} fusion(f32[256,32,32,1]{0,2,3,1:T(8,128)S(1)} %bitcast.69, f32[2,16,16,256]{3,2,1,0:T(8,128)} %copy-done.1), kind=kOutput, calls=%fused_computation.2 | convolution fusion | flops 805306368 | bytes 2359296 | tf_op jit(solution)/shard_map/abk,kcd->acbd/dot_general | solution.py:12
  75.4 2.4 %copy.24 = f32[16,32,16,32]{3,2,1,0:T(8,128)} copy(f32[16,32,16,32]{3,2,0,1:T(8,128)S(1)} %convolution_bitcast_fusion) | data formatting | bytes 2097152 | tf_op jit(solution)/shard_map/abk,kcd->acbd/transpose | solution.py:12
  77.8 3.5 %squeeze_stack_reshape.7 = f32[512,512]{1,0:T(8,128)S(1)} reshape(f32[16,32,16,32]{3,2,1,0:T(8,128)} %copy.24) | data formatting | bytes 2097152 | tf_op jit(solution)/shard_map/squeeze;stack;reshape | solution.py:37
  81.3 5.6 %compare_and_fusion = (pred[512]{0:T(512)(128)(4,1)S(1)}, s32[512]{0:T(512)S(1)}) fusion(s32[]{:T(128)} %bitcast.30, s32[]{:T(128)} %bitcast.29, s32[]{:T(128)} %bitcast.28, s32[]{:T(128)} %bitcast.27, s32[]{:T(128)} %bitcast.26, s32[]{:T(128)} %bitcast.25, s32[]{:T(128)} %bitcast.24, s32[]{:T(128)} %bitcast.23, s32[]{:T(128)} %bitcast.22), kind=kLoop, calls=%fused_computation.29 | loop fusion | flops 20992 | bytes 2596 | tf_op jit(solution)/shard_map/jit(_take)/and | solution.py:22
  87.0 1.6 %gather_fusion.1 = f32[512,512]{1,0:T(8,128)S(1)} fusion(f32[512,512]{1,0:T(8,128)S(1)} %squeeze_stack_reshape.7, s32[1024]{0:T(1024)S(1)} %pad_clamp_fusion), kind=kCustom, calls=%fused_computation.1.clone | custom fusion | bytes 2099200 | tf_op jit(solution)/shard_map/jit(_take)/gather | solution.py:22
  88.6 0.0 all-to-all-done.1
  88.6 3.1 %convolution_bitcast_fusion.2 = f32[1,512,512]{2,1,0:T(8,128)} fusion(f32[512,512]{1,0:T(8,128)S(1)} %bitcast.66, f32[512,512]{1,0:T(8,128)S(1)} %gather_fusion.1, pred[512]{0:T(512)(128)(4,1)S(1)} %get-tuple-element.6), kind=kOutput, calls=%fused_computation.4 | convolution fusion | flops 1610874880 | bytes 3146240 | tf_op jit(solution)/shard_map/dot_general | solution.py:45
  (2 shorter events, 0.0 us)
Async XLA Ops:
  2.3 9.5 %copy-start.2 = (f32[2,4,16,256]{3,2,1,0:T(8,128)S(1)}, f32[2,4,16,256]{3,2,1,0:T(8,128)}, u32[]{:S(2)}) copy-start(f32[2,4,16,256]{3,2,1,0:T(8,128)} %param.7) | copy-start | bytes 393220
  2.3 60.9 %all-to-all-start = ((f32[8,4,64,128]{3,2,0,1:T(8,128)}), f32[8,4,64,128]{3,2,0,1:T(8,128)S(1)}, u32[]{:S(2)}, u32[]{:S(2)}) async-start(f32[8,4,64,128]{3,2,0,1:T(8,128)} %copy.20), calls=%async_computation | async-start | bytes 2097152 | tf_op jit(solution)/shard_map/all_to_all | solution.py:41
  44.9 0.8 copy-start.1
  51.6 3.6 %copy-start.3 = (s32[2,9]{1,0:T(2,128)S(1)}, s32[2,9]{1,0:T(2,128)}, u32[]{:S(2)}) copy-start(s32[2,9]{1,0:T(2,128)} %param.9) | copy-start | bytes 220
  63.2 7.5 %copy-start = (f32[1,256,1024]{2,1,0:T(8,128)S(1)}, f32[1,256,1024]{2,1,0:T(8,128)}, u32[]{:S(2)}) copy-start(f32[1,256,1024]{2,1,0:T(8,128)} %get-tuple-element.10) | copy-start | bytes 3145732
  66.9 21.7 %all-to-all-start.1 = ((f32[8,1,64,512]{3,2,1,0:T(8,128)}), f32[8,1,64,512]{3,2,1,0:T(8,128)S(1)}, u32[]{:S(2)}, u32[]{:S(2)}) async-start(f32[8,1,64,512]{3,2,1,0:T(8,128)} %bitcast.20), calls=%async_computation.1 | async-start | bytes 2097152 | tf_op jit(solution)/shard_map/all_to_all | solution.py:43
where the time goes:
time: 92.3 us; the launch traced here: 91.7 us
  blocking collectives  33.1 us (36%)
  local copies, waits for them, and re-layouts  23.1 us (25%)
  matrix products  13.9 us (15%)
  other arithmetic  11.3 us (12%)
  starting transfers between devices  10.2 us (11%)
    all_gather x1, blocking collectives, on_device(): whole_left = lax.all_gather(left_factors, 'grp', axis=1, tiled=True)  33.1 us
    and x2, other arithmetic, relabel(): return jnp.take(branch, source_rows, axis=0)  11.3 us
    dot_general x2, matrix products, assemble(): jnp.einsum('abk,kcd->acbd', left, table, precision=lax.Precision.HIGHEST)  7.84 us
    all_to_all x1, starting transfers between devices, on_device(): lax.all_to_all(shaped, 'grp', split_axis=1, concat_axis=3, tiled=True)  6.48 us
    transpose x2, local copies, waits for them, and re-layouts, assemble(): jnp.einsum('abk,kcd->acbd', left, table, precision=lax.Precision.HIGHEST)  4.82 us
    all_to_all x1, starting transfers between devices, on_device(): lax.all_to_all(halfway, 'stem', split_axis=0, concat_axis=2, tiled=True)  3.74 us
    another operation x1, local copies, waits for them, and re-layouts, on_device(): branch_one = relabel(branches[0], index_labels[0])  3.56 us
    another operation x1, local copies, waits for them, and re-layouts, on_device(): branch_two = relabel(branches[1], index_labels[1])  3.54 us
  transfers between devices with their start and end apart: 2, of which 0 were waited for; matrix products, arithmetic and copies ran while one was open for 42% of the time, Pallas kernels for 0%

commit v1 on v0

--- a/solution.py
+++ b/solution.py
@@ -29,7 +29,14 @@
 
 
 def on_device(stem_tensor, left_factors, right_factors, index_labels):
-    whole_left = lax.all_gather(left_factors, "grp", axis=1, tiled=True)
+    n_dev_all = lax.axis_size("grp")
+    reached = [None] * n_dev_all
+    reached[n_dev_all - 1] = left_factors
+    panels = tuple(((dev_j, (dev_j + 1) % n_dev_all) for dev_j in range(n_dev_all)))
+    for tick in range(n_dev_all - 2, -1, -1):
+        reached[tick] = lax.ppermute(reached[tick + 1], "grp", perm=panels)
+    field_out = jnp.concatenate(reached, 1)
+    whole_left = jnp.roll(field_out, (lax.axis_index("grp") + 1) * left_factors.shape[1], axis=1)
     branches = jnp.stack(
         [assemble(whole_left[branch_id], right_factors[branch_id]) for branch_id in range(2)]
     )

time: 92.3 us -> 85.1 us (0.922)
  blocking collectives: 33.1 us -> 0 us
  waiting for transfers between devices: 0.01 us -> 18.2 us
  starting transfers between devices: 10.2 us -> 16 us
  matrix products: 13.9 us -> 18.3 us
  local copies, waits for them, and re-layouts: 23.1 us -> 20.3 us
    all_gather x1 -> x0, blocking collectives: 33.1 us -> none  [on_device(): whole_left = lax.all_gather(left_factors, 'grp', axis=1, tiled=True)]
    ppermute x0 -> x3, waiting for transfers between devices: none -> 18.2 us  [on_device(): reached[tick] = lax.ppermute(reached[tick + 1], 'grp', perm=panels)]
    ppermute x0 -> x3, starting transfers between devices: none -> 8.3 us  [on_device(): reached[tick] = lax.ppermute(reached[tick + 1], 'grp', perm=panels)]
    transpose x2 -> x0, local copies, waits for them, and re-layouts: 4.82 us -> none  [assemble(): jnp.einsum('abk,kcd->acbd', left, table, precision=lax.Precision.HIGHEST)]
    dot_general x2, matrix products: 7.84 us -> 12.3 us  [assemble(): jnp.einsum('abk,kcd->acbd', left, table, precision=lax.Precision.HIGHEST)]
    all_to_all x1, starting transfers between devices: 6.48 us -> 3.99 us  [on_device(): lax.all_to_all(shaped, 'grp', split_axis=1, concat_axis=3, tiled=True)]
    unnamed x8 -> x15, local copies, waits for them, and re-layouts: 0.84 us -> 2.9 us
  transfers between devices with their start and end apart: 2 -> 5, of which waited for: 0 -> 1; matrix products, arithmetic and copies ran while one was open for 42% -> 50% of each run, Pallas kernels for 0% -> 0%
where the time goes in v1:
time: 85.1 us; the launch traced here: 84.3 us
  local copies, waits for them, and re-layouts  20.3 us (24%)
  matrix products  18.3 us (22%)
  waiting for transfers between devices  18.2 us (21%)
  starting transfers between devices  16 us (19%)
  other arithmetic  11.1 us (13%)
    ppermute x3, waiting for transfers between devices, on_device(): reached[tick] = lax.ppermute(reached[tick + 1], 'grp', perm=panels)  18.2 us
    dot_general x2, matrix products, assemble(): jnp.einsum('abk,kcd->acbd', left, table, precision=lax.Precision.HIGHEST)  12.3 us
    and x2, other arithmetic, relabel(): return jnp.take(branch, source_rows, axis=0)  11.1 us
    ppermute x3, starting transfers between devices, on_device(): reached[tick] = lax.ppermute(reached[tick + 1], 'grp', perm=panels)  8.3 us
    all_to_all x1, starting transfers between devices, on_device(): lax.all_to_all(shaped, 'grp', split_axis=1, concat_axis=3, tiled=True)  3.99 us
    all_to_all x1, starting transfers between devices, on_device(): lax.all_to_all(halfway, 'stem', split_axis=0, concat_axis=2, tiled=True)  3.74 us
    another operation x1, local copies, waits for them, and re-layouts, on_device(): branch_two = relabel(branches[1], index_labels[1])  3.54 us
    another operation x1, local copies, waits for them, and re-layouts, on_device(): branch_one = relabel(branches[0], index_labels[0])  3.54 us
  transfers between devices with their start and end apart: 5, of which 1 were waited for; matrix products, arithmetic and copies ran while one was open for 50% of the time, Pallas kernels for 0%

profile of v1, /device:TPU:0, one launch (start us, length us, event | category | flops | bytes accessed | tf_op | source)
XLA Modules:
  0.0 84.3 jit_solution(15639400047145776291)
XLA Ops:
  0.0 3.1 %collective-permute-start = (f32[2,4,16,256]{3,2,1,0:T(8,128)}, f32[2,4,16,256]{3,2,1,0:T(8,128)S(1)}, u32[]{:S(2)}, u32[]{:S(2)}) collective-permute-start(f32[2,4,16,256]{3,2,1,0:T(8,128)} %param.7), channel_id=1, source_target_pairs={{0,1},{1,2},{2,3},{3,0},{4,5},{5,6},{6,7},{7,4},{8,9},{9,10},{10,1... | collective-permute-start | bytes 393224 | tf_op jit(solution)/shard_map/ppermute | solution.py:37
  3.1 0.0 copy-start.3
  3.1 2.3 %copy.15 = f32[8,4,64,128]{3,2,0,1:T(8,128)} copy(f32[8,4,64,128]{3,2,1,0:T(8,128)} %bitcast.70) | data formatting | bytes 2097152 | tf_op jit(solution)/shard_map/reshape | solution.py:47
  5.4 0.0 copy-start.1
  5.4 4.0 %all-to-all-start = ((f32[8,4,64,128]{3,2,0,1:T(8,128)}), f32[8,4,64,128]{3,2,0,1:T(8,128)S(1)}, u32[]{:S(2)}, u32[]{:S(2)}) async-start(f32[8,4,64,128]{3,2,0,1:T(8,128)} %copy.15), calls=%async_computation | async-start | bytes 2097152 | tf_op jit(solution)/shard_map/all_to_all | solution.py:48
  9.4 0.0 collective-permute-done
  9.4 2.0 %collective-permute-start.1 = (f32[2,4,16,256]{3,2,1,0:T(8,128)S(1)}, f32[2,4,16,256]{3,2,1,0:T(8,128)S(1)}, u32[]{:S(2)}, u32[]{:S(2)}) collective-permute-start(f32[2,4,16,256]{3,2,1,0:T(8,128)S(1)} %collective-permute-done), channel_id=1, source_target_pairs={{0,1},{1,2},{2,3},{3,0},{4,5},{5,6},{6,7},{7,4},{8,9},{9,10},{10,1... | collective-permute-start | bytes 393224 | tf_op jit(solution)/shard_map/ppermute | solution.py:37
  11.4 2.7 %fusion.13 = (f32[1,256,1024]{2,1,0:T(8,128)}, f32[1,256,1024]{2,1,0:T(8,128)S(1)}) fusion(f32[2,256,1024]{2,1,0:T(8,128)} %param.8), kind=kLoop, calls=%fused_computation.43 | loop fusion | bytes 4194304 | tf_op jit(solution)/shard_map/slice | solution.py:41
  14.1 0.0 copy-done.3
  14.1 0.7 fusion.14
  14.8 18.2 %collective-permute-done.1 = f32[2,4,16,256]{3,2,1,0:T(8,128)S(1)} collective-permute-done((f32[2,4,16,256]{3,2,1,0:T(8,128)S(1)}, f32[2,4,16,256]{3,2,1,0:T(8,128)S(1)}, u32[]{:S(2)}, u32[]{:S(2)}) %collective-permute-start.1) | collective-permute-done | bytes 131104 | tf_op jit(solution)/shard_map/ppermute | solution.py:37
  33.0 3.2 %collective-permute-start.2 = (f32[2,4,16,256]{3,2,1,0:T(8,128)S(1)}, f32[2,4,16,256]{3,2,1,0:T(8,128)}, u32[]{:S(2)}, u32[]{:S(2)}) collective-permute-start(f32[2,4,16,256]{3,2,1,0:T(8,128)S(1)} %collective-permute-done.1), channel_id=1, source_target_pairs={{0,1},{1,2},{2,3},{3,0},{4,5},{5,6},{6,7},{7,4},{8,9},{9,10},{10,1... | collective-permute-start | bytes 393224 | tf_op jit(solution)/shard_map/ppermute | solution.py:37
  36.3 5.6 %compare_and_fusion.1 = (pred[512]{0:T(512)(128)(4,1)S(1)}, s32[512]{0:T(512)S(1)}) fusion(s32[]{:T(128)} %bitcast.8, s32[]{:T(128)} %bitcast.7, s32[]{:T(128)} %bitcast.6, s32[]{:T(128)} %bitcast.5, s32[]{:T(128)} %bitcast.4, s32[]{:T(128)} %bitcast.3, s32[]{:T(128)} %bitcast.2, s32[]{:T(128)} %bitcast.1, s32[]{:T(128)} %bitcast), kind=kLoop, calls=%fused_computation.38 | loop fusion | flops 20992 | bytes 2596 | tf_op jit(solution)/shard_map/jit(_take)/and | solution.py:22
  41.9 0.3 copy.14
  42.2 0.0 collective-permute-done.2
  42.2 0.9 %constant_dynamic-update-slice_fusion.7 = f32[2,32,16,256]{3,2,1,0:T(8,128)S(1)} fusion(f32[2,4,16,256]{3,2,1,0:T(8,128)} %collective-permute-done.2), kind=kLoop, calls=%fused_computation.23 | loop fusion | bytes 262144
  43.2 0.0 copy-done.1
  43.2 0.9 %constant_dynamic-update-slice_fusion.3 = f32[2,32,16,256]{3,2,1,0:T(8,128)S(1)} fusion(f32[2,32,16,256]{3,2,1,0:T(8,128)S(1)} %constant_dynamic-update-slice_fusion.4, f32[2,4,16,256]{3,2,1,0:T(8,128)} %collective-permute-done.2), kind=kLoop, calls=%fused_computation.19 | loop fusion | bytes 262144
  44.2 0.0 copy-start.2
  44.2 1.0 %copy-done.2 = f32[2,32,16,256]{3,2,1,0:T(8,128)} copy-done((f32[2,32,16,256]{3,2,1,0:T(8,128)}, f32[2,32,16,256]{3,2,1,0:T(8,128)S(1)}, u32[]{:S(2)}) %copy-start.2) | copy-done | bytes 1048600
  45.2 5.0 %convolution_bitcast_fusion.1 = f32[16,32,16,32]{3,2,1,0:T(8,128)} fusion(f32[256,32,32,1]{0,2,1,3:T(8,128)S(1)} %bitcast.68, f32[2,32,16,256]{3,2,1,0:T(8,128)S(1)} %constant_dynamic-update-slice_fusion, s32[]{:T(128)S(6)} %select_n.21), kind=kOutput, calls=%fused_computation.3 | convolution fusion | flops 805306368 | bytes 2359300 | tf_op jit(solution)/shard_map/abk,kcd->acbd/dot_general | solution.py:12
  50.2 3.5 %squeeze_stack_reshape.6 = f32[512,512]{1,0:T(8,128)S(1)} reshape(f32[16,32,16,32]{3,2,1,0:T(8,128)} %convolution_bitcast_fusion.1) | data formatting | bytes 2097152 | tf_op jit(solution)/shard_map/squeeze;stack;reshape | solution.py:43
  53.8 1.6 %gather_fusion = f32[512,512]{1,0:T(8,128)S(1)} fusion(f32[512,512]{1,0:T(8,128)S(1)} %squeeze_stack_reshape.6, s32[1024]{0:T(1024)S(1)} %pad_clamp_fusion.1), kind=kCustom, calls=%fused_computation.clone | custom fusion | bytes 2099200 | tf_op jit(solution)/shard_map/jit(_take)/gather | solution.py:22
  55.4 0.0 copy-start
  55.4 0.0 all-to-all-done
  55.4 0.7 copy.16
  56.1 3.0 %fusion = f32[512,512]{0,1:T(8,128)} fusion(f32[64,8,4,128]{3,2,1,0:T(4,128)S(1)} %bitcast.67, f32[512,512]{1,0:T(8,128)S(1)} %gather_fusion, pred[512]{0:T(512)(128)(4,1)S(1)} %get-tuple-element.8), kind=kOutput, calls=%fused_computation.5 | convolution fusion | flops 1610874880 | bytes 3146240 | tf_op jit(solution)/shard_map/dot_general | solution.py:27
  59.1 3.7 %all-to-all-start.1 = ((f32[8,1,64,512]{3,2,1,0:T(8,128)}), f32[8,1,64,512]{3,2,1,0:T(8,128)S(1)}, u32[]{:S(2)}, u32[]{:S(2)}) async-start(f32[8,1,64,512]{3,2,1,0:T(8,128)} %bitcast.20), calls=%async_computation.1 | async-start | bytes 2097152 | tf_op jit(solution)/shard_map/all_to_all | solution.py:50
  62.8 0.0 copy-done
  62.9 0.3 copy.18
  63.2 5.5 %compare_and_fusion = (pred[512]{0:T(512)(128)(4,1)S(1)}, s32[512]{0:T(512)S(1)}) fusion(s32[]{:T(128)} %bitcast.30, s32[]{:T(128)} %bitcast.29, s32[]{:T(128)} %bitcast.28, s32[]{:T(128)} %bitcast.27, s32[]{:T(128)} %bitcast.26, s32[]{:T(128)} %bitcast.25, s32[]{:T(128)} %bitcast.24, s32[]{:T(128)} %bitcast.23, s32[]{:T(128)} %bitcast.22), kind=kLoop, calls=%fused_computation.37 | loop fusion | flops 20992 | bytes 2596 | tf_op jit(solution)/shard_map/jit(_take)/and | solution.py:22
  68.7 7.3 %convolution_bitcast_fusion = f32[16,32,16,32]{3,2,1,0:T(8,128)} fusion(f32[256,32,32,1]{0,2,1,3:T(8,128)S(1)} %bitcast.69, f32[2,32,16,256]{3,2,1,0:T(8,128)} %copy-done.2, s32[]{:T(128)S(6)} %add.92, s32[]{:T(128)S(6)} %select_n.21), kind=kOutput, calls=%fused_computation.2 | convolution fusion | flops 805306368 | bytes 2359304 | tf_op jit(solution)/shard_map/abk,kcd->acbd/dot_general | solution.py:12
  76.0 3.5 %squeeze_stack_reshape.7 = f32[512,512]{1,0:T(8,128)S(1)} reshape(f32[16,32,16,32]{3,2,1,0:T(8,128)} %convolution_bitcast_fusion) | data formatting | bytes 2097152 | tf_op jit(solution)/shard_map/squeeze;stack;reshape | solution.py:44
  79.6 1.6 %gather_fusion.1 = f32[512,512]{1,0:T(8,128)S(1)} fusion(f32[512,512]{1,0:T(8,128)S(1)} %squeeze_stack_reshape.7, s32[1024]{0:T(1024)S(1)} %pad_clamp_fusion), kind=kCustom, calls=%fused_computation.1.clone | custom fusion | bytes 2099200 | tf_op jit(solution)/shard_map/jit(_take)/gather | solution.py:22
  81.2 0.0 all-to-all-done.1
  81.2 3.1 %convolution_bitcast_fusion.2 = f32[1,512,512]{2,1,0:T(8,128)} fusion(f32[512,512]{1,0:T(8,128)S(1)} %bitcast.66, f32[512,512]{1,0:T(8,128)S(1)} %gather_fusion.1, pred[512]{0:T(512)(128)(4,1)S(1)} %get-tuple-element.6), kind=kOutput, calls=%fused_computation.4 | convolution fusion | flops 1610874880 | bytes 3146240 | tf_op jit(solution)/shard_map/dot_general | solution.py:52
  (8 shorter events, 0.1 us)
Async XLA Ops:
  0.0 9.4 %collective-permute-start = (f32[2,4,16,256]{3,2,1,0:T(8,128)}, f32[2,4,16,256]{3,2,1,0:T(8,128)S(1)}, u32[]{:S(2)}, u32[]{:S(2)}) collective-permute-start(f32[2,4,16,256]{3,2,1,0:T(8,128)} %param.7), channel_id=1, source_target_pairs={{0,1},{1,2},{2,3},{3,0},{4,5},{5,6},{6,7},{7,4},{8,9},{9,10},{10,1... | collective-permute-start | bytes 393224 | tf_op jit(solution)/shard_map/ppermute | solution.py:37
  3.1 11.0 %copy-start.3 = (s32[2,9]{1,0:T(2,128)S(1)}, s32[2,9]{1,0:T(2,128)}, u32[]{:S(2)}) copy-start(s32[2,9]{1,0:T(2,128)} %param.9) | copy-start | bytes 220
  5.4 37.8 %copy-start.1 = (f32[2,4,16,256]{3,2,1,0:T(8,128)S(1)}, f32[2,4,16,256]{3,2,1,0:T(8,128)}, u32[]{:S(2)}) copy-start(f32[2,4,16,256]{3,2,1,0:T(8,128)} %param.7) | copy-start | bytes 393220
  5.4 50.0 %all-to-all-start = ((f32[8,4,64,128]{3,2,0,1:T(8,128)}), f32[8,4,64,128]{3,2,0,1:T(8,128)S(1)}, u32[]{:S(2)}, u32[]{:S(2)}) async-start(f32[8,4,64,128]{3,2,0,1:T(8,128)} %copy.15), calls=%async_computation | async-start | bytes 2097152 | tf_op jit(solution)/shard_map/all_to_all | solution.py:48
  9.4 23.7 %collective-permute-start.1 = (f32[2,4,16,256]{3,2,1,0:T(8,128)S(1)}, f32[2,4,16,256]{3,2,1,0:T(8,128)S(1)}, u32[]{:S(2)}, u32[]{:S(2)}) collective-permute-start(f32[2,4,16,256]{3,2,1,0:T(8,128)S(1)} %collective-permute-done), channel_id=1, source_target_pairs={{0,1},{1,2},{2,3},{3,0},{4,5},{5,6},{6,7},{7,4},{8,9},{9,10},{10,1... | collective-permute-start | bytes 393224 | tf_op jit(solution)/shard_map/ppermute | solution.py:37
  33.0 9.2 %collective-permute-start.2 = (f32[2,4,16,256]{3,2,1,0:T(8,128)S(1)}, f32[2,4,16,256]{3,2,1,0:T(8,128)}, u32[]{:S(2)}, u32[]{:S(2)}) collective-permute-start(f32[2,4,16,256]{3,2,1,0:T(8,128)S(1)} %collective-permute-done.1), channel_id=1, source_target_pairs={{0,1},{1,2},{2,3},{3,0},{4,5},{5,6},{6,7},{7,4},{8,9},{9,10},{10,1... | collective-permute-start | bytes 393224 | tf_op jit(solution)/shard_map/ppermute | solution.py:37
  44.2 1.0 %copy-start.2 = (f32[2,32,16,256]{3,2,1,0:T(8,128)}, f32[2,32,16,256]{3,2,1,0:T(8,128)S(1)}, u32[]{:S(2)}) copy-start(f32[2,32,16,256]{3,2,1,0:T(8,128)S(1)} %constant_dynamic-update-slice_fusion) | copy-start | bytes 3145732
  55.4 7.5 %copy-start = (f32[1,256,1024]{2,1,0:T(8,128)S(1)}, f32[1,256,1024]{2,1,0:T(8,128)}, u32[]{:S(2)}) copy-start(f32[1,256,1024]{2,1,0:T(8,128)} %get-tuple-element.10) | copy-start | bytes 3145732
  59.1 22.1 %all-to-all-start.1 = ((f32[8,1,64,512]{3,2,1,0:T(8,128)}), f32[8,1,64,512]{3,2,1,0:T(8,128)S(1)}, u32[]{:S(2)}, u32[]{:S(2)}) async-start(f32[8,1,64,512]{3,2,1,0:T(8,128)} %bitcast.20), calls=%async_computation.1 | async-start | bytes 2097152 | tf_op jit(solution)/shard_map/all_to_all | solution.py:50
